TPU v7x, 256 devices: a whole 4x4x8 slice. The times are simulated.
256 devices in a mesh: blk: 16 (over z, x_hi), leaf: 8 (over y, core), rhs: 2 (over x_lo).
Axes of the slice: x: 4 (x_hi: 2, x_lo: 2; x = x_hi * 2 + x_lo), y: 4, z: 8, core: 2. Of those that a mesh axis runs over, the one named last changes fastest.
Arguments:
- residual: float32 [32, 8, 65536], P('rhs', 'leaf', 'blk'), may hold values from -160 to 160
- points: float32 [3, 8, 65536], P(None, 'leaf', 'blk'), may hold values from -12330 to 12330
- noise: float32 [8, 65536], P('leaf', 'blk'), may hold values from 1 to 2
- block_list: int32 [8, 8, 256], P('leaf'), may hold values from 0 to 1, as said below
Outputs:
- correction: float32 [32, 8, 65536], P('rhs', 'leaf', 'blk')
- new_residual: float32 [32, 8, 65536], P('rhs', 'leaf', 'blk')
- basis: float32 [128, 8, 65536], P('rhs', 'leaf', 'blk')
Inputs may be any that keep to these rules, and one draw needn't show every extreme that they name: The list is symmetric: block_list[t, k, i] == block_list[t, 7 - k, (i + d) mod 256] with d the offset of entry k.
All inputs are finite; a program needn't handle non-finite values.
Results may differ from a plain program's by a relative error of at most 0.007.
Values sent between devices are 32-bit elements; how exact they have to be, the bound alone decides.
A program may use at most 128 MiB of HBM per device.

v0:
```python
import jax
import jax.numpy as jnp
from jax import lax
from jax.sharding import PartitionSpec as P

M = 32
S = 4
BS = 256
REACH = 4
SUPPORT = 1408
centre_shift = 1.5
amplitude = 1.1
exact = lax.Precision.HIGHEST


def extended(x, sides, width):
    for axis, dim in sides:
        count, length = (lax.axis_size(axis), x.shape[dim])
        up = [(i, (i + 1) % count) for i in range(count)]
        down = [(j, i) for i, j in up]
        last = lax.slice_in_dim(x, length - width, length, axis=dim)
        leading = lax.slice_in_dim(x, 0, width, axis=dim)
        before = lax.ppermute(last, axis, up)
        after = lax.ppermute(leading, axis, down)
        x = jnp.concatenate([before, x, after], axis=dim)
    return x


def kernel_tile(near_points, own_points):
    squared = (near_points[0][:, None] - own_points[0][None, :]) ** 2
    squared = squared + (near_points[1][:, None] - own_points[1][None, :]) ** 2
    squared = squared + (near_points[2][:, None] - own_points[2][None, :]) ** 2
    radius = jnp.sqrt(squared) / SUPPORT
    remain = jnp.maximum(1.0 - radius, 0.0)
    return remain * remain * (remain * remain) * (4.0 * radius + 1.0) * (amplitude / SUPPORT)


def band_product(field_wide, points_wide, weights, rows_out):
    per_turn = rows_out // 8
    count = field_wide.shape[0]

    def turn(carry, index):
        pieces = []
        for inner in range(per_turn):
            block = index * per_turn + inner
            own_points = lax.dynamic_slice_in_dim(points_wide, (block + REACH) * BS, BS, 1)
            total = jnp.zeros((count, BS), jnp.float32)
            for offset in range(2 * REACH + 1):
                column_at = (block + offset) * BS
                near_points = lax.dynamic_slice_in_dim(points_wide, column_at, BS, 1)
                near_field = lax.dynamic_slice_in_dim(field_wide, column_at, BS, 1)
                listed = lax.dynamic_index_in_dim(weights[offset], block, 0, False)
                tile = kernel_tile(near_points, own_points) * listed
                total = total + jnp.dot(near_field, tile, precision=exact)
            pieces.append(total)
        return (carry, jnp.concatenate(pieces, axis=1))

    carry, parts = lax.scan(turn, jnp.zeros((), jnp.int32), jnp.arange(8, dtype=jnp.int32))
    return jnp.moveaxis(parts, 0, 1).reshape(count, rows_out * BS)


def galerkin(gram, count_points, count_sides):
    normed = gram / count_points
    basis_count = normed.shape[0]
    gram_basis = normed[:basis_count, :basis_count]
    factor_low = jnp.linalg.cholesky(gram_basis)
    inverse_low = lax.linalg.triangular_solve(
        factor_low, jnp.eye(basis_count, dtype=jnp.float32), left_side=True, lower=True
    )
    cross = normed[:basis_count, count_sides:] + centre_shift * gram_basis
    projected = jnp.dot(
        jnp.dot(inverse_low, cross, precision=exact), inverse_low.T, precision=exact
    )
    projected = 0.5 * (projected + projected.T)
    small_side = jnp.dot(inverse_low, gram_basis[:, :count_sides], precision=exact)
    proj_factor = jnp.linalg.cholesky(projected)
    halfway = lax.linalg.triangular_solve(proj_factor, small_side, left_side=True, lower=True)
    coeffs = lax.linalg.triangular_solve(
        proj_factor, halfway, left_side=True, lower=True, transpose_a=True
    )
    combo = jnp.dot(coeffs.T, inverse_low, precision=exact)
    return (inverse_low, combo)


def row_products(rows, cols):
    return lax.dot_general(rows, cols, (((1,), (1,)), ((), ())), precision=exact)


def butterfly_sum(x, axes):
    for axis in axes:
        count = lax.axis_size(axis)
        if count & count - 1:
            x = lax.psum(x, axis)
            continue
        step = 1
        while step < count:
            x = x + lax.ppermute(x, axis, [(i, i ^ step) for i in range(count)])
            step *= 2
    return x


def local(residual, points, noise, block_list):
    field = residual[:, 0]
    coords = points[:, 0]
    nugget = noise[0]
    own_rows = field.shape[1]
    own_blocks = own_rows // BS
    first_block = lax.axis_index("blk") * own_blocks
    listed = block_list[0].astype(jnp.float32)
    nine = jnp.concatenate(
        [listed[:REACH], jnp.ones((1, listed.shape[1]), jnp.float32), listed[REACH:]], axis=0
    )
    margin = S * REACH
    wrapped = jnp.concatenate([nine[:, -margin:], nine, nine[:, :margin]], axis=1)
    powers = [field]
    rim = REACH * BS
    coords_wide = extended(coords, (("blk", 1),), rim)
    own_weights = lax.dynamic_slice_in_dim(wrapped, first_block + margin, own_blocks, 1)
    current = field
    for power_step in range(S):
        widened = extended(current, (("blk", 1),), rim)
        current = (
            band_product(widened, coords_wide, own_weights, own_blocks)
            + (nugget - centre_shift) * current
        )
        powers.append(current)
    half_panel = jnp.stack(powers, axis=0)
    count_points = own_rows * lax.axis_size("blk") * lax.axis_size("leaf")
    sides_here = field.shape[0]
    whole = lax.all_gather(half_panel, "rhs", axis=1, tiled=True)
    flat = whole.reshape(-1, own_rows)
    gram = butterfly_sum(row_products(flat[: S * M], flat), ("leaf", "blk"))
    inverse_low, combo = galerkin(gram, count_points, M)
    first_rows = flat[: S * M]
    image = flat[M:] + centre_shift * first_rows
    part = lax.axis_index("rhs")
    basis_here = S * M // lax.axis_size("rhs")
    mine_low = lax.dynamic_slice_in_dim(inverse_low, part * basis_here, basis_here, 0)
    mine_combo = lax.dynamic_slice_in_dim(combo, part * sides_here, sides_here, 0)
    correction = jnp.dot(mine_combo, first_rows, precision=exact)
    new_residual = field - jnp.dot(mine_combo, image, precision=exact)
    basis = jnp.dot(mine_low, first_rows, precision=exact)
    return (correction[:, None], new_residual[:, None], basis[:, None])


def solution(mesh):
    placed = (
        P("rhs", "leaf", "blk"),
        P(None, "leaf", "blk"),
        P("leaf", "blk"),
        P("leaf", None, None),
    )
    return jax.shard_map(
        local,
        mesh=mesh,
        in_specs=placed,
        out_specs=(P("rhs", "leaf", "blk"), P("rhs", "leaf", "blk"), P("rhs", "leaf", "blk")),
        check_vma=False,
    )
```

profile of v0, /device:TPU:8, one launch (start us, length us, event | category | flops | bytes accessed | tf_op | source)
XLA Modules:
  0.0 1043.5 jit_solution(11603520780824057718)
XLA Ops:
  7.2 1.1 copy.44
  8.3 8.4 collective-permute-start.1
  16.7 0.8 copy.45
  17.6 5.7 collective-permute-start.3
  23.3 1.1 bitcast_dynamic-update-slice_fusion
  24.4 0.7 convert_element_type.5
  25.2 0.7 broadcast_add_fusion
  26.0 4.6 collective-permute-done.2
  30.8 209.0 %while.52 = (s32[]{:T(128)}, f32[8,16,512]{2,1,0:T(8,128)S(1)}, s32[8]{0:T(128)S(1)}, f32[16,6144]{1,0:T(8,128)S(1)}, f32[3,6144]{1,0:T(4,128)S(1)}, /*index=5*/...) while((s32[]{:T(128)}, f32[8,16,512]{2,1,0:T(8,128)S(1)}, ...), condition=%wide.region_1.2_spmd, body=%wide.region_0.1_spmd.sunk | while | flops 246620224 | bytes 1092197 | solution.py:58
  240.3 1.3 collective-permute-start.5
  241.6 2.5 collective-permute-start.4
  244.3 2.1 collective-permute-done.5
  246.3 3.1 collective-permute-done.4
  249.6 208.9 %while.53 = (s32[]{:T(128)}, f32[8,16,512]{2,1,0:T(8,128)S(1)}, s32[8]{0:T(128)S(1)}, f32[16,6144]{1,0:T(8,128)S(1)}, f32[3,6144]{1,0:T(4,128)S(1)}, /*index=5*/...) while((s32[]{:T(128)}, f32[8,16,512]{2,1,0:T(8,128)S(1)}, ...), condition=%wide.region_3.4_spmd, body=%wide.region_2.3_spmd.sunk | while | flops 246620224 | bytes 1092197 | solution.py:58
  458.9 3.9 collective-permute-start.6
  462.8 1.8 collective-permute-done.7
  464.6 2.6 collective-permute-done.6
  467.3 208.6 %while.54 = (s32[]{:T(128)}, f32[8,16,512]{2,1,0:T(8,128)S(1)}, s32[8]{0:T(128)S(1)}, f32[16,6144]{1,0:T(8,128)S(1)}, f32[3,6144]{1,0:T(4,128)S(1)}, /*index=5*/...) while((s32[]{:T(128)}, f32[8,16,512]{2,1,0:T(8,128)S(1)}, ...), condition=%wide.region_5.6_spmd, body=%wide.region_4.5_spmd.sunk | while | flops 246620224 | bytes 1092197 | solution.py:58
  676.3 3.7 collective-permute-start.8
  680.1 2.0 collective-permute-done.9
  682.1 2.4 collective-permute-done.8
  684.5 209.2 %while.55 = (s32[]{:T(128)}, f32[8,16,512]{2,1,0:T(8,128)S(1)}, s32[8]{0:T(128)S(1)}, f32[16,6144]{1,0:T(8,128)S(1)}, f32[3,6144]{1,0:T(4,128)S(1)}, /*index=5*/...) while((s32[]{:T(128)}, f32[8,16,512]{2,1,0:T(8,128)S(1)}, ...), condition=%wide.region_7.8_spmd, body=%wide.region_6.7_spmd.sunk | while | flops 246620224 | bytes 1092197 | solution.py:58
  894.1 1.1 copy-done.3
  895.1 39.7 %all-gather.2.cloned.1.call-done = f32[5,32,4096]{2,1,0:T(8,128)} async-done(((f32[5,16,4096]{2,1,0:T(8,128)}), f32[5,32,4096]{2,1,0:T(8,128)}) %all-gather.2.cloned.1.call-update) | async-done | bytes 2621456 | tf_op jit(solution)/shard_map/all_gather | solution.py:130
  934.8 4.1 fusion.2570
  938.9 2.2 fusion.2577
  941.2 1.3 collective-permute-done.10
  943.1 4.0 collective-permute-done.11
  947.1 2.2 collective-permute-start.12
  949.3 3.8 collective-permute-done.12
  953.2 3.0 collective-permute-start.13
  956.2 3.3 collective-permute-done.13
  959.4 1.6 collective-permute-start.14
  961.1 3.8 collective-permute-done.14
  964.9 2.0 collective-permute-start.15
  966.8 4.3 collective-permute-done.15
  971.2 6.3 collective-permute-start.16
  977.5 3.2 bitcast_add_fusion
  980.8 11.7 %cholesky.44 = f32[128,128]{1,0:T(8,128)S(1)} custom-call(f32[128,128]{1,0:T(8,128)S(1)} %fusion.2546), custom_call_target="Cholesky" | custom-call | tf_op jit(solution)/shard_map/jit(cholesky)/cholesky | solution.py:66
  993.9 9.8 custom-call.10
  1004.9 11.7 %cholesky.55 = f32[128,128]{1,0:T(8,128)S(1)} custom-call(f32[128,128]{1,0:T(8,128)S(1)} %fusion.2542), custom_call_target="Cholesky" | custom-call | tf_op jit(solution)/shard_map/jit(cholesky)/cholesky | solution.py:76
  1018.0 10.0 custom-call.11
  1028.8 1.1 convolution_bitcast_fusion.1
  1029.9 1.0 copy.26
  1030.9 1.1 fusion.2532
  1032.0 1.0 copy.27
  1033.0 1.2 convolution_bitcast_fusion
  1034.2 2.0 copy.28
  (951 shorter events, 414.0 us)
Async XLA Ops:
  7.2 927.7 %all-gather.2.cloned.1.call-start = ((), (), s32[]{:S(2)}) async-start(), calls=%async_computation | async-start | bytes 3932160 | tf_op jit(solution)/shard_map/all_gather | solution.py:130
  8.3 22.3 %collective-permute-start.1 = (f32[16,1024]{1,0:T(8,128)S(1)}, f32[16,1024]{1,0:T(8,128)S(1)}, u32[]{:S(2)}, u32[]{:S(2)}) collective-permute-start(f32[16,1024]{1,0:T(8,128)S(1)} %get-tuple-element.897), channel_id=1, source_target_pairs={{16,0},{32,16},{48,32},{64,48},{80,64},{96,80},{112,96},{128,112},... | collective-permute-start | bytes 196616 | tf_op jit(solution)/shard_map/ppermute | solution.py:24
  16.7 14.0 %collective-permute-start = (f32[16,1024]{1,0:T(8,128)S(1)}, f32[16,1024]{1,0:T(8,128)S(1)}, u32[]{:S(2)}, u32[]{:S(2)}) collective-permute-start(f32[16,1024]{1,0:T(8,128)S(1)} %get-tuple-element.896), channel_id=1, source_target_pairs={{0,16},{16,32},{32,48},{48,64},{64,80},{80,96},{96,112},{112,128},... | collective-permute-start | bytes 196616 | tf_op jit(solution)/shard_map/ppermute | solution.py:23
  17.6 8.5 collective-permute-start.3
  23.3 7.4 collective-permute-start.2
  30.8 209.3 %copy-start.2 = (f32[16,1,4096]{2,1,0:T(1,128)S(1)}, f32[16,1,4096]{2,1,0:T(1,128)}, u32[]{:S(2)}) copy-start(f32[16,1,4096]{2,1,0:T(1,128)} %param.13) | copy-start | bytes 786436
  240.3 6.1 collective-permute-start.5
  241.6 7.9 collective-permute-start.4
  458.8 5.8 collective-permute-start.7
  458.9 8.4 collective-permute-start.6
  676.2 5.8 collective-permute-start.9
  676.3 8.1 collective-permute-start.8
  894.1 1.1 copy-start.3
  934.8 4.1 copy-start
  941.1 1.4 collective-permute-start.10
  942.5 4.6 collective-permute-start.11
  947.1 6.0 collective-permute-start.12
  953.2 6.2 collective-permute-start.13
  959.4 5.4 collective-permute-start.14
  964.9 6.3 collective-permute-start.15
  971.2 9.5 collective-permute-start.16
  1028.0 2.8 copy-start.1
Sparse Core Ops, SparseCore 0:
  895.3 39.5 all-gather.1
where the time goes:
time: 1060 us; the launch traced here: 1040 us
  loops' own time  429 us (40%)
  matrix products  279 us (26%)
  local copies, waits for them, and re-layouts  147 us (14%)
  waiting for transfers between devices  78.7 us (7%)
  other arithmetic  52.4 us (5%)
  starting transfers between devices  41.6 us (4%)
  between operations  15 us (1%)
    another operation x4, loops' own time, band_product(): lax.scan(turn, jnp.zeros((), jnp.int32), jnp.arange(8, dtype=jnp.int32))  429 us
    dot_general x576, matrix products, turn(): total = total + jnp.dot(near_field, tile, precision=exact)  272 us
    dynamic_slice x160, local copies, waits for them, and re-layouts, turn(): listed = lax.dynamic_index_in_dim(weights[offset], block, 0, False)  109 us
    all_gather x1, waiting for transfers between devices, local(): whole = lax.all_gather(half_panel, 'rhs', axis=1, tiled=True)  39.7 us
  transfers between devices with their start and end apart: 18, of which 14 were waited for; matrix products, arithmetic and copies ran while one was open for 1% of the time, Pallas kernels for 0%

commit v1 on v0

--- a/solution.py
+++ b/solution.py
@@ -127,7 +127,8 @@
     half_panel = jnp.stack(powers, axis=0)
     count_points = own_rows * lax.axis_size("blk") * lax.axis_size("leaf")
     sides_here = field.shape[0]
-    whole = lax.all_gather(half_panel, "rhs", axis=1, tiled=True)
+    repeated = jnp.stack([half_panel] * lax.axis_size("rhs"))
+    whole = jnp.concatenate(lax.all_to_all(repeated, "rhs", 0, 0), axis=1)
     flat = whole.reshape(-1, own_rows)
     gram = butterfly_sum(row_products(flat[: S * M], flat), ("leaf", "blk"))
     inverse_low, combo = galerkin(gram, count_points, M)

time: 1060 us -> 1020 us (0.962)
  waiting for transfers between devices: 78.7 us -> 27.4 us
  blocking collectives: 0 us -> 29.1 us
  between operations: 15 us -> 1.65 us
    all_gather x1 -> x0, waiting for transfers between devices: 39.7 us -> none  [local(): whole = lax.all_gather(half_panel, 'rhs', axis=1, tiled=True)]
    all_to_all x0 -> x1, blocking collectives: none -> 29.1 us  [local(): whole = jnp.concatenate(lax.all_to_all(repeated, 'rhs', 0, 0), axis=1)]
    ppermute x5, starting transfers between devices: 15.6 us -> 28.6 us  [extended(): after = lax.ppermute(leading, axis, down)]
  transfers between devices with their start and end apart: 18 -> 17, of which waited for: 14 -> 11; matrix products, arithmetic and copies ran while one was open for 1% -> 1% of each run, Pallas kernels for 0% -> 0%
where the time goes in v1:
time: 1020 us; the launch traced here: 1010 us
  loops' own time  429 us (42%)
  matrix products  279 us (27%)
  local copies, waits for them, and re-layouts  144 us (14%)
  other arithmetic  51.1 us (5%)
  starting transfers between devices  45.3 us (4%)
  blocking collectives  29.1 us (3%)
  waiting for transfers between devices  27.4 us (3%)
    another operation x4, loops' own time, band_product(): lax.scan(turn, jnp.zeros((), jnp.int32), jnp.arange(8, dtype=jnp.int32))  429 us
    dot_general x576, matrix products, turn(): total = total + jnp.dot(near_field, tile, precision=exact)  272 us
    dynamic_slice x160, local copies, waits for them, and re-layouts, turn(): listed = lax.dynamic_index_in_dim(weights[offset], block, 0, False)  107 us
    all_to_all x1, blocking collectives, local(): whole = jnp.concatenate(lax.all_to_all(repeated, 'rhs', 0, 0), axis=1)  29.1 us
    ppermute x5, starting transfers between devices, extended(): after = lax.ppermute(leading, axis, down)  28.6 us
    ppermute x7, waiting for transfers between devices, butterfly_sum(): x = x + lax.ppermute(x, axis, [(i, i ^ step) for i in range(count)])  22.5 us
  transfers between devices with their start and end apart: 17, of which 11 were waited for; matrix products, arithmetic and copies ran while one was open for 1% of the time, Pallas kernels for 0%

profile of v1, /device:TPU:8, one launch (start us, length us, event | category | flops | bytes accessed | tf_op | source)
XLA Modules:
  0.0 1006.6 jit_solution(8588473101267761764)
XLA Ops:
  0.6 0.8 copy.48
  1.5 3.1 collective-permute-start.2
  4.6 5.4 collective-permute-start.3
  10.0 1.1 copy.47
  11.2 5.6 collective-permute-start.1
  16.8 1.1 bitcast_dynamic-update-slice_fusion
  17.9 0.7 convert_element_type.5
  18.7 0.7 broadcast_add_fusion
  19.7 208.2 %while.52 = (s32[]{:T(128)}, f32[8,16,512]{2,1,0:T(8,128)S(1)}, s32[8]{0:T(128)S(1)}, f32[16,6144]{1,0:T(8,128)S(1)}, f32[3,6144]{1,0:T(4,128)S(1)}, /*index=5*/...) while((s32[]{:T(128)}, f32[8,16,512]{2,1,0:T(8,128)S(1)}, ...), condition=%wide.region_1.2_spmd, body=%wide.region_0.1_spmd.sunk | while | flops 246620224 | bytes 1092189 | solution.py:58
  228.2 5.9 collective-permute-start.5
  234.5 1.6 collective-permute-done.4
  236.1 208.9 %while.53 = (s32[]{:T(128)}, f32[8,16,512]{2,1,0:T(8,128)S(1)}, s32[8]{0:T(128)S(1)}, f32[16,6144]{1,0:T(8,128)S(1)}, f32[3,6144]{1,0:T(4,128)S(1)}, /*index=5*/...) while((s32[]{:T(128)}, f32[8,16,512]{2,1,0:T(8,128)S(1)}, ...), condition=%wide.region_3.4_spmd, body=%wide.region_2.3_spmd.sunk | while | flops 246620224 | bytes 1092189 | solution.py:58
  445.3 6.4 collective-permute-start.7
  451.9 1.5 collective-permute-done.6
  453.6 207.4 %while.54 = (s32[]{:T(128)}, f32[8,16,512]{2,1,0:T(8,128)S(1)}, s32[8]{0:T(128)S(1)}, f32[16,6144]{1,0:T(8,128)S(1)}, f32[3,6144]{1,0:T(4,128)S(1)}, /*index=5*/...) while((s32[]{:T(128)}, f32[8,16,512]{2,1,0:T(8,128)S(1)}, ...), condition=%wide.region_5.6_spmd, body=%wide.region_4.5_spmd.sunk | while | flops 246620224 | bytes 1092189 | solution.py:58
  661.1 0.9 collective-permute-start.8
  662.0 5.4 collective-permute-start.9
  667.7 1.7 collective-permute-done.8
  669.4 208.7 %while.55 = (s32[]{:T(128)}, f32[8,16,512]{2,1,0:T(8,128)S(1)}, s32[8]{0:T(128)S(1)}, f32[16,6144]{1,0:T(8,128)S(1)}, f32[3,6144]{1,0:T(4,128)S(1)}, /*index=5*/...) while((s32[]{:T(128)}, f32[8,16,512]{2,1,0:T(8,128)S(1)}, ...), condition=%wide.region_7.8_spmd, body=%wide.region_6.7_spmd.sunk | while | flops 246620224 | bytes 1092189 | solution.py:58
  673.3 0.7 constant_dynamic-slice_fusion.156
  699.4 0.7 constant_dynamic-slice_fusion.156
  725.5 0.7 constant_dynamic-slice_fusion.156
  878.7 29.1 %all_to_all.5 = f32[2,5,16,4096]{3,2,1,0:T(8,128)S(1)} all-to-all(f32[2,5,16,4096]{3,2,1,0:T(8,128)S(1)} %pad_maximum_fusion), channel_id=1, replica_groups=mesh['blk'=16,'leaf'=8,'rhs'=2] {'rhs'}, dimensions={0} | all-to-all | bytes 5242880 | tf_op jit(solution)/shard_map/all_to_all | solution.py:131
  907.8 1.8 fusion.2570
  910.0 2.2 fusion.2577
  912.3 1.3 collective-permute-done.10
  914.1 4.1 collective-permute-done.11
  918.2 2.4 collective-permute-start.12
  920.6 3.6 collective-permute-done.12
  924.3 5.9 collective-permute-done.13
  930.3 1.4 collective-permute-start.14
  931.6 3.2 collective-permute-done.14
  934.8 4.4 collective-permute-start.15
  939.2 1.7 copy.28
  941.0 1.0 collective-permute-done.15
  942.0 3.6 collective-permute-start.16
  945.5 1.6 bitcast_add_fusion
  947.1 3.5 collective-permute-done.16
  950.7 11.7 %cholesky.44 = f32[128,128]{1,0:T(8,128)S(1)} custom-call(f32[128,128]{1,0:T(8,128)S(1)} %fusion.2546), custom_call_target="Cholesky" | custom-call | tf_op jit(solution)/shard_map/jit(cholesky)/cholesky | solution.py:66
  963.8 9.8 custom-call.10
  974.3 1.2 convolution_bitcast_fusion
  975.6 2.0 copy.31
  978.1 12.0 %cholesky.55 = f32[128,128]{1,0:T(8,128)S(1)} custom-call(f32[128,128]{1,0:T(8,128)S(1)} %fusion.2542), custom_call_target="Cholesky" | custom-call | tf_op jit(solution)/shard_map/jit(cholesky)/cholesky | solution.py:76
  991.4 9.8 custom-call.11
  1002.0 1.1 convolution_bitcast_fusion.1
  1003.1 1.1 fusion.2532
  1004.2 1.0 copy.30
  1005.2 1.0 copy.29
  (949 shorter events, 410.5 us)
Async XLA Ops:
  1.5 18.1 %collective-permute-start.2 = (f32[3,1024]{1,0:T(4,128)S(1)}, f32[3,1024]{1,0:T(4,128)S(1)}, u32[]{:S(2)}, u32[]{:S(2)}) collective-permute-start(f32[3,1024]{1,0:T(4,128)S(1)} %get-tuple-element.898), channel_id=1, source_target_pairs={{0,16},{16,32},{32,48},{48,64},{64,80},{80,96},{96,112},{112,128},... | collective-permute-start | bytes 36872 | tf_op jit(solution)/shard_map/ppermute | solution.py:23
  4.6 15.0 %collective-permute-start.3 = (f32[3,1024]{1,0:T(4,128)S(1)}, f32[3,1024]{1,0:T(4,128)S(1)}, u32[]{:S(2)}, u32[]{:S(2)}) collective-permute-start(f32[3,1024]{1,0:T(4,128)S(1)} %get-tuple-element.899), channel_id=1, source_target_pairs={{16,0},{32,16},{48,32},{64,48},{80,64},{96,80},{112,96},{128,112},... | collective-permute-start | bytes 36872 | tf_op jit(solution)/shard_map/ppermute | solution.py:24
  11.1 8.5 collective-permute-start
  11.2 8.4 collective-permute-start.1
  19.7 208.2 %copy-start.1 = (f32[16,1,4096]{2,1,0:T(1,128)S(1)}, f32[16,1,4096]{2,1,0:T(1,128)}, u32[]{:S(2)}) copy-start(f32[16,1,4096]{2,1,0:T(1,128)} %param.13) | copy-start | bytes 786436
  228.1 8.0 collective-permute-start.4
  228.2 7.9 collective-permute-start.5
  445.2 8.2 collective-permute-start.6
  445.3 8.3 collective-permute-start.7
  661.1 8.3 collective-permute-start.8
  662.0 7.4 collective-permute-start.9
  912.2 1.4 collective-permute-start.10
  913.6 4.6 collective-permute-start.11
  918.2 6.0 collective-permute-start.12
  924.2 6.0 collective-permute-start.13
  930.3 4.5 collective-permute-start.14
  934.8 7.1 collective-permute-start.15
  942.0 8.6 collective-permute-start.16
  1001.2 1.9 copy-start
